TPU v7x, 256 devices: a whole 4x4x8 slice. The times are simulated.
256 devices in a mesh: ctx: 32 (over z_hi, x, core), tp: 8 (over y, z_lo).
Axes of the slice: x: 4, y: 4, z: 8 (z_hi: 4, z_lo: 2; z = z_hi * 2 + z_lo), core: 2. Of those that a mesh axis runs over, the one named last changes fastest.
Arguments:
- features: bfloat16 [16384, 3, 4096], P('ctx', None, 'tp'), may hold values from -6 to 6
- short_filter: float32 [3, 7, 4096], P(None, None, 'tp'), may hold values from -2 to 2
- decay_rate: float32 [16, 4096], P(None, 'tp'), may hold values from 0 to 1, as said below
- residue: float32 [16, 4096], P(None, 'tp'), may hold values from -2 to 2
- skip_gain: float32 [4096], P('tp'), may hold values from -4 to 4
- norm_gain: float32 [4096], replicated, may hold values from 0.1 to 1.9
- qkv_weight: bfloat16 [4096, 3, 2048], P('ctx', None, 'tp'), may hold values from -2 to 2
Outputs:
- mixer: bfloat16 [16384, 4096], P('ctx', 'tp')
- attended: bfloat16 [16384, 2048], P('ctx', 'tp')
Inputs may be any that keep to these rules, and one draw needn't show every extreme that they name: `decay_rate`: decay rates are positive.
All inputs are finite; a program needn't handle non-finite values.
Results may differ from a plain program's by a relative error of at most 0.01.
Values may be sent and summed in bfloat16 or wider, within the bound.
No kernel may reach another device: no remote copies, remote signals or barrier semaphores. Data moves between devices by JAX's collectives and lax.ppermute only.
A program may use at most 128 MiB of HBM per device.

v0:
```python
from functools import reduce
import math
import jax
import jax.numpy as jnp
from jax import lax
from jax.sharding import PartitionSpec as P

HD = 128
TAPS = 7
WINDOW = 3
CHUNK = 128
EPSILON = 1e-06
PRECISE = lax.Precision.HIGHEST


def to_bf16_grid(value):
    return lax.reduce_precision(value, exponent_bits=8, mantissa_bits=7)


def from_behind(value, axis, steps):
    count = lax.axis_size(axis)
    leading, last = (max(0, -steps), min(count, count - steps))
    return lax.ppermute(value, axis, [(source, source + steps) for source in range(leading, last)])


def local_modal_conv(signal, decay, mixing):
    tokens, channels = signal.shape
    modes = decay.shape[0]
    chunks = tokens // CHUNK
    centre = (CHUNK - 1) / 2.0
    offsets = jnp.arange(CHUNK, dtype=jnp.float32) - centre
    up = jnp.exp(offsets[:, None, None] * decay[None])
    down = jnp.exp(-offsets[:, None, None] * decay[None])
    after = jnp.exp(-(jnp.arange(CHUNK, dtype=jnp.float32) + 1.0)[:, None, None] * decay[None])
    tri = (jnp.arange(CHUNK)[:, None] >= jnp.arange(CHUNK)[None, :]).astype(jnp.float32)
    blocks = signal.reshape(chunks, CHUNK, channels)
    lifted = (up[None] * blocks[:, :, None, :]).reshape(chunks, CHUNK, modes * channels)
    summed = jnp.einsum("ts,qsk->qtk", tri, lifted, precision=PRECISE).reshape(
        chunks, CHUNK, modes, channels
    )
    states = down[None] * summed
    intra = jnp.sum(states * mixing[None, None], axis=2)
    ends = states[:, CHUNK - 1]
    step = jnp.exp(-float(CHUNK) * decay)
    carry = jnp.zeros_like(decay)
    entering = []
    for chunk in range(chunks):
        entering.append(carry)
        carry = step * carry + ends[chunk]
    entering = jnp.stack(entering)
    weighted_after = after * mixing[None]
    return (intra, entering, carry, weighted_after)


def on_device(features, short_filter, decay_rate, residue, skip_gain, norm_gain, qkv_weight):
    tok_dev, _, channels = features.shape
    head_cols = qkv_weight.shape[2]
    shard_rows = lax.all_gather(qkv_weight, "ctx", axis=0, tiled=True)
    rim_rows = features[tok_dev - (TAPS - 1) :]
    before = from_behind(rim_rows, "ctx", 1)
    extended = jnp.concatenate([before, features], axis=0).astype(jnp.float32)
    short_conv = jnp.zeros((tok_dev, 3, channels), jnp.float32)
    for offset in range(TAPS):
        first_row = TAPS - 1 - offset
        short_conv = (
            short_conv
            + short_filter[:, offset, :][None] * extended[first_row : first_row + tok_dev]
        )
    gated = to_bf16_grid(short_conv[:, 1] * short_conv[:, 2])
    mixing = residue * jnp.sqrt(decay_rate)
    intra, entering, block_end, weighted_after = local_modal_conv(gated, decay_rate, mixing)
    block_step = jnp.exp(-float(tok_dev) * decay_rate)
    history = from_behind(block_end, "ctx", 1)
    factor = block_step
    count = lax.axis_size("ctx")
    shift = 1
    while shift < count:
        history = history + factor * from_behind(history, "ctx", shift)
        factor = factor * factor
        shift *= 2
    chunks = tok_dev // CHUNK
    chunk_step = jnp.exp(-float(CHUNK) * decay_rate)
    lead = [jnp.ones_like(decay_rate)]
    for chunk in range(1, chunks):
        lead.append(lead[-1] * chunk_step)
    lead = jnp.stack(lead)
    total_state = entering + lead * history[None]
    carried = jnp.einsum("lnc,qnc->qlc", weighted_after, total_state, precision=PRECISE)
    filtered = (intra + carried).reshape(tok_dev, channels) + skip_gain[None] * gated
    filtered = to_bf16_grid(filtered)
    mixer = (short_conv[:, 0] * filtered).astype(jnp.bfloat16)
    gathered = lax.all_gather(mixer, "tp", axis=1, tiled=True)
    as_float = gathered.astype(jnp.float32)
    inverse = lax.rsqrt(jnp.mean(as_float * as_float, axis=1, keepdims=True) + EPSILON)
    normed = (as_float * inverse * norm_gain[None]).astype(jnp.bfloat16)
    flat_rows = shard_rows.reshape(shard_rows.shape[0], 3 * head_cols)
    projected = jnp.dot(normed, flat_rows, preferred_element_type=jnp.float32).astype(jnp.bfloat16)
    heads = head_cols // HD
    query = projected[:, :head_cols].reshape(tok_dev, heads, HD)
    kv_pair = projected[:, head_cols:]
    blocks_kv = [kv_pair] + [from_behind(kv_pair, "ctx", lag) for lag in range(1, WINDOW)]
    position = lax.axis_index("ctx")
    row_ids = jnp.arange(tok_dev)
    causal = row_ids[:, None] >= row_ids[None, :]
    score_list = []
    for lag_step in range(WINDOW):
        keys = blocks_kv[lag_step][:, :head_cols].reshape(tok_dev, heads, HD)
        scores = jnp.einsum(
            "thd,shd->hts", query, keys, preferred_element_type=jnp.float32
        ) / math.sqrt(HD)
        if lag_step == 0:
            allowed = causal
        else:
            allowed = jnp.broadcast_to(position >= lag_step, causal.shape)
        score_list.append(jnp.where(allowed[None], scores, -jnp.inf))
    peak = reduce(jnp.maximum, [jnp.max(entry, axis=2) for entry in score_list])
    total = jnp.zeros((heads, tok_dev), jnp.float32)
    output = jnp.zeros((tok_dev, heads, HD), jnp.float32)
    for lag_step in range(WINDOW):
        expo = jnp.exp(score_list[lag_step] - peak[:, :, None])
        total = total + jnp.sum(expo, axis=2)
        values = blocks_kv[lag_step][:, head_cols:].reshape(tok_dev, heads, HD)
        output = output + jnp.einsum(
            "hts,shd->thd", expo.astype(jnp.bfloat16), values, preferred_element_type=jnp.float32
        )
    attended = (output / total.T[:, :, None]).astype(jnp.bfloat16).reshape(tok_dev, head_cols)
    return (mixer, attended)


def solution(mesh):
    placed = (
        P("ctx", None, "tp"),
        P(None, None, "tp"),
        P(None, "tp"),
        P(None, "tp"),
        P("tp"),
        P(),
        P("ctx", None, "tp"),
    )
    return jax.shard_map(
        on_device,
        mesh=mesh,
        in_specs=placed,
        out_specs=(P("ctx", "tp"), P("ctx", "tp")),
        check_vma=False,
    )
```

profile of v0, /device:TPU:105, one launch (start us, length us, event | category | flops | bytes accessed | tf_op | source)
XLA Modules:
  0.0 396.7 jit_solution(14588440854774348517)
XLA Ops:
  8.0 3.7 collective-permute-start
  15.3 4.6 %multiply_exponential_fusion = f32[128,8192]{0,1:T(8,128)} fusion(f32[8192]{0:T(1024)S(1)} %bitcast.158, f32[128]{0:T(128)S(1)} %iota_add_fusion), kind=kLoop, calls=%fused_computation.15 | loop fusion | flops 1048576 | bytes 4227584 | tf_op jit(solution)/shard_map/exp | solution.py:32
  19.9 3.6 multiply_exponential_fusion.1
  23.5 5.8 %copy.51 = f32[128,16,512]{2,1,0:T(8,128)} copy(f32[128,16,512]{0,1,2:T(8,128)} %multiply_exponential_fusion.1) | data formatting | bytes 8388608 | tf_op jit(solution)/shard_map/exp | solution.py:33
  29.8 2.6 fusion.11
  33.6 2.5 copy.52
  36.1 9.5 %bitcast_multiply_fusion = f32[4,128,8192]{1,2,0:T(8,128)} fusion(f32[4,128,512]{1,2,0:T(8,128)} %copy.52, f32[128,8192]{0,1:T(8,128)} %multiply_exponential_fusion), kind=kLoop, calls=%fused_computation | loop fusion | flops 4194304 | bytes 22020096 | tf_op jit(solution)/shard_map/mul | solution.py:37
  45.6 14.5 %fusion.78 = f32[4,8192,128]{2,1,0:T(8,128)} fusion(f32[4,128,8192]{1,2,0:T(8,128)} %bitcast_multiply_fusion), kind=kOutput, calls=%fused_computation.102 | convolution fusion | flops 6442467328 | bytes 33554432 | tf_op jit(solution)/shard_map/ts,qsk->qtk/dot_general | solution.py:38
  60.1 19.9 %copy.53 = f32[4,128,16,512]{3,2,1,0:T(8,128)} copy(f32[4,128,16,512]{1,3,2,0:T(8,128)} %bitcast.151) | data formatting | bytes 33554432 | tf_op jit(solution)/shard_map/reshape | solution.py:38
  80.0 10.5 %multiply_reduce_fusion = (f32[4,128,512]{2,1,0:T(8,128)}, f32[4,128,16,512]{3,2,1,0:T(8,128)S(1)}) fusion(f32[16,512]{1,0:T(8,128)S(1)} %sqrt_multiply_fusion, f32[4,128,16,512]{3,2,1,0:T(8,128)} %copy.53, f32[128,16,512]{2,1,0:T(8,128)} %copy.51), kind=kLoop, calls=%fused_computation.1 | loop fusion | flops 12320768 | bytes 38830080 | tf_op jit(solution)/shard_map/reduce_sum | solution.py:42
  94.2 4.0 %collective-permute-start.2 = (f32[16,512]{1,0:T(8,128)S(1)}, f32[16,512]{1,0:T(8,128)S(1)}, u32[]{:S(2)}, u32[]{:S(2)}) collective-permute-start(f32[16,512]{1,0:T(8,128)S(1)} %collective-permute-done.1), channel_id=1, source_target_pairs={{0,8},{8,16},{16,24},{24,32},{32,40},{40,48},{48,56},{56,64},{64,7... | collective-permute-start | bytes 98312 | tf_op jit(solution)/shard_map/ppermute | solution.py:23
  98.3 2.6 collective-permute-done.2
  100.9 2.1 collective-permute-start.3
  103.0 6.0 %collective-permute-done.3 = f32[16,512]{1,0:T(8,128)S(1)} collective-permute-done((f32[16,512]{1,0:T(8,128)S(1)}, f32[16,512]{1,0:T(8,128)S(1)}, u32[]{:S(2)}, u32[]{:S(2)}) %collective-permute-start.3) | collective-permute-done | bytes 32800 | tf_op jit(solution)/shard_map/ppermute | solution.py:23
  109.0 5.1 %collective-permute-start.4 = (f32[16,512]{1,0:T(8,128)S(1)}, f32[16,512]{1,0:T(8,128)S(1)}, u32[]{:S(2)}, u32[]{:S(2)}) collective-permute-start(f32[16,512]{1,0:T(8,128)S(1)} %multiply_add_fusion.3), channel_id=1, source_target_pairs={{0,32},{8,40},{16,48},{24,56},{32,64},{40,72},{48,80},{56,88},{64,... | collective-permute-start | bytes 98312 | tf_op jit(solution)/shard_map/ppermute | solution.py:23
  114.2 2.8 collective-permute-done.4
  117.0 8.7 %collective-permute-start.5 = (f32[16,512]{1,0:T(8,128)S(1)}, f32[16,512]{1,0:T(8,128)S(1)}, u32[]{:S(2)}, u32[]{:S(2)}) collective-permute-start(f32[16,512]{1,0:T(8,128)S(1)} %multiply_add_fusion.2), channel_id=1, source_target_pairs={{0,64},{8,72},{16,80},{24,88},{32,96},{40,104},{48,112},{56,120},{... | collective-permute-start | bytes 98312 | tf_op jit(solution)/shard_map/ppermute | solution.py:23
  126.8 4.9 %collective-permute-start.6 = (f32[16,512]{1,0:T(8,128)S(1)}, f32[16,512]{1,0:T(8,128)}, u32[]{:S(2)}, u32[]{:S(2)}) collective-permute-start(f32[16,512]{1,0:T(8,128)S(1)} %multiply_add_fusion.1), channel_id=1, source_target_pairs={{0,128},{8,136},{16,144},{24,152},{32,160},{40,168},{48,176},{56,1... | collective-permute-start | bytes 98312 | tf_op jit(solution)/shard_map/ppermute | solution.py:23
  132.5 2.5 copy.56
  137.4 2.2 copy.55
  139.6 7.4 %fusion.35 = f32[4,128,512]{1,0,2:T(4,128)} fusion(f32[4,128,512]{1,0,2:T(4,128)} %copy.56, f32[4,16,512]{1,0,2:T(4,128)} %copy.55, f32[16,512]{0,1:T(8,128)} %copy.54, f32[128]{0:T(128)S(1)} %add_negate_fusion, f32[16,512]{0,1:T(8,128)S(1)} %copy.50), kind=kOutput, calls=%fused_computation.51 | convolution fusion | flops 52690944 | bytes 2294272 | tf_op jit(solution)/shard_map/lnc,qnc->qlc/dot_general | solution.py:88
  147.1 2.6 copy.75
  149.6 2.6 fusion.47
  153.2 102.1 %all-gather.3.cloned.1.call-done = bf16[512,4096]{1,0:T(8,128)(2,1)} async-done(((bf16[512,512]{1,0:T(8,128)(2,1)}), bf16[512,4096]{1,0:T(8,128)(2,1)}) %all-gather.3.cloned.1.call-update) | async-done | bytes 4194320 | tf_op jit(solution)/shard_map/all_gather | solution.py:92
  255.4 3.1 fusion
  258.5 74.5 %all-gather.5.cloned.1.call-done = bf16[4096,3,256]{0,2,1:T(8,128)(2,1)} async-done(((bf16[128,3,256]{0,2,1:T(8,128)(2,1)}), bf16[4096,3,256]{0,2,1:T(8,128)(2,1)}) %all-gather.5.cloned.1.call-update) | async-done | bytes 6291472 | tf_op jit(solution)/shard_map/all_gather | solution.py:58
  332.9 7.5 %fusion.29 = bf16[512,768]{1,0:T(8,128)(2,1)S(1)} fusion(bf16[4096,768]{0,1:T(8,128)(2,1)} %bitcast.160, bf16[512,4096]{1,0:T(8,128)(2,1)} %all-gather.3.cloned.1.call-done, f32[4096]{0:T(1024)S(1)} %copy-done.6, f32[512]{0:T(512)S(1)} %add_rsqrt_fusion), kind=kOutput, calls=%fused_computation.49 | convolution fusion | flops 3230007296 | bytes 11290624 | tf_op jit(solution)/shard_map/dot_general | solution.py:97
  340.5 3.2 collective-permute-start.7
  343.8 3.3 collective-permute-start.8
  349.9 2.8 collective-permute-done.7
  352.9 28.8 %collective-permute-done.8 = bf16[512,512]{1,0:T(8,128)(2,1)S(1)} collective-permute-done((bf16[512,512]{1,0:T(8,128)(2,1)S(1)}, bf16[512,512]{1,0:T(8,128)(2,1)S(1)}, u32[]{:S(2)}, u32[]{:S(2)}) %collective-permute-start.8) | collective-permute-done | bytes 524320 | tf_op jit(solution)/shard_map/ppermute | solution.py:23
  383.5 2.5 fusion.43
  (66 shorter events, 23.6 us)
Async XLA Ops:
  7.2 248.2 %all-gather.3.cloned.1.call-start = ((), (), s32[]{:S(2)}) async-start(), calls=%async_computation | async-start | bytes 4718592 | tf_op jit(solution)/shard_map/all_gather | solution.py:92
  8.0 21.4 %collective-permute-start = (bf16[6,3,512]{2,0,1:T(8,128)(2,1)S(1)}, bf16[6,3,512]{2,0,1:T(8,128)(2,1)S(1)}, u32[]{:S(2)}, u32[]{:S(2)}) collective-permute-start(bf16[6,3,512]{2,0,1:T(8,128)(2,1)S(1)} %slice.102), channel_id=1, source_target_pairs={{0,8},{8,16},{16,24},{24,32},{32,40},{40,48},{48,56},{56,64},{64,7... | collective-permute-start | bytes 55304 | tf_op jit(solution)/shard_map/ppermute | solution.py:23
  23.5 5.8 %copy-start.2 = (bf16[512,3,512]{2,0,1:T(8,128)(2,1)S(1)}, bf16[512,3,512]{2,0,1:T(8,128)(2,1)}, u32[]{:S(2)}) copy-start(bf16[512,3,512]{2,0,1:T(8,128)(2,1)} %param.7) | copy-start | bytes 4718596
  80.0 10.5 %copy-start = (f32[16,512]{1,0:T(8,128)S(1)}, f32[16,512]{1,0:T(8,128)}, u32[]{:S(2)}) copy-start(f32[16,512]{1,0:T(8,128)} %param.9) | copy-start | bytes 98308
  91.1 3.1 collective-permute-start.1
  94.2 6.6 %collective-permute-start.2 = (f32[16,512]{1,0:T(8,128)S(1)}, f32[16,512]{1,0:T(8,128)S(1)}, u32[]{:S(2)}, u32[]{:S(2)}) collective-permute-start(f32[16,512]{1,0:T(8,128)S(1)} %collective-permute-done.1), channel_id=1, source_target_pairs={{0,8},{8,16},{16,24},{24,32},{32,40},{40,48},{48,56},{56,64},{64,7... | collective-permute-start | bytes 98312 | tf_op jit(solution)/shard_map/ppermute | solution.py:23
  100.9 8.2 %collective-permute-start.3 = (f32[16,512]{1,0:T(8,128)S(1)}, f32[16,512]{1,0:T(8,128)S(1)}, u32[]{:S(2)}, u32[]{:S(2)}) collective-permute-start(f32[16,512]{1,0:T(8,128)S(1)} %multiply_add_fusion.4), channel_id=1, source_target_pairs={{0,16},{8,24},{16,32},{24,40},{32,48},{40,56},{48,64},{56,72},{64,... | collective-permute-start | bytes 98312 | tf_op jit(solution)/shard_map/ppermute | solution.py:23
  109.0 8.0 %collective-permute-start.4 = (f32[16,512]{1,0:T(8,128)S(1)}, f32[16,512]{1,0:T(8,128)S(1)}, u32[]{:S(2)}, u32[]{:S(2)}) collective-permute-start(f32[16,512]{1,0:T(8,128)S(1)} %multiply_add_fusion.3), channel_id=1, source_target_pairs={{0,32},{8,40},{16,48},{24,56},{32,64},{40,72},{48,80},{56,88},{64,... | collective-permute-start | bytes 98312 | tf_op jit(solution)/shard_map/ppermute | solution.py:23
  117.0 9.8 %collective-permute-start.5 = (f32[16,512]{1,0:T(8,128)S(1)}, f32[16,512]{1,0:T(8,128)S(1)}, u32[]{:S(2)}, u32[]{:S(2)}) collective-permute-start(f32[16,512]{1,0:T(8,128)S(1)} %multiply_add_fusion.2), channel_id=1, source_target_pairs={{0,64},{8,72},{16,80},{24,88},{32,96},{40,104},{48,112},{56,120},{... | collective-permute-start | bytes 98312 | tf_op jit(solution)/shard_map/ppermute | solution.py:23
  126.8 8.3 %collective-permute-start.6 = (f32[16,512]{1,0:T(8,128)S(1)}, f32[16,512]{1,0:T(8,128)}, u32[]{:S(2)}, u32[]{:S(2)}) collective-permute-start(f32[16,512]{1,0:T(8,128)S(1)} %multiply_add_fusion.1), channel_id=1, source_target_pairs={{0,128},{8,136},{16,144},{24,152},{32,160},{40,168},{48,176},{56,1... | collective-permute-start | bytes 98312 | tf_op jit(solution)/shard_map/ppermute | solution.py:23
  139.6 10.0 %copy-start.5 = (f32[512]{0:T(512)S(1)}, f32[512]{0:T(512)}, u32[]{:S(2)}) copy-start(f32[512]{0:T(512)} %param.11) | copy-start | bytes 6148
  149.6 2.7 copy-start.4
  152.2 180.7 %copy-start.6 = (f32[4096]{0:T(1024)S(1)}, f32[4096]{0:T(1024)}, u32[]{:S(2)}) copy-start(f32[4096]{0:T(1024)} %param.12) | copy-start | bytes 49156
  152.2 180.7 %all-gather.5.cloned.1.call-start = ((), (), s32[]{:S(2)}) async-start(), calls=%async_computation.1 | async-start | bytes 6488064 | tf_op jit(solution)/shard_map/all_gather | solution.py:58
  340.5 12.2 %collective-permute-start.7 = (bf16[512,512]{1,0:T(8,128)(2,1)S(1)}, bf16[512,512]{1,0:T(8,128)(2,1)S(1)}, u32[]{:S(2)}, u32[]{:S(2)}) collective-permute-start(bf16[512,512]{1,0:T(8,128)(2,1)S(1)} %slice.148), channel_id=1, source_target_pairs={{0,8},{8,16},{16,24},{24,32},{32,40},{40,48},{48,56},{56,64},{64,7... | collective-permute-start | bytes 1572872 | tf_op jit(solution)/shard_map/ppermute | solution.py:23
  343.8 38.0 %collective-permute-start.8 = (bf16[512,512]{1,0:T(8,128)(2,1)S(1)}, bf16[512,512]{1,0:T(8,128)(2,1)S(1)}, u32[]{:S(2)}, u32[]{:S(2)}) collective-permute-start(bf16[512,512]{1,0:T(8,128)(2,1)S(1)} %slice.148), channel_id=1, source_target_pairs={{0,16},{8,24},{16,32},{24,40},{32,48},{40,56},{48,64},{56,72},{64,... | collective-permute-start | bytes 1572872 | tf_op jit(solution)/shard_map/ppermute | solution.py:23
  383.1 3.0 copy-start.1
  387.4 1.0 copy-start.3
Sparse Core Ops, SparseCore 0:
  152.4 102.9 all-gather.2
  258.4 74.4 all-gather.4
where the time goes:
time: 398 us; the launch traced here: 397 us
  waiting for transfers between devices  222 us (56%)
  local copies, waits for them, and re-layouts  44.1 us (11%)
  other arithmetic  43.3 us (11%)
  starting transfers between devices  37.1 us (9%)
  matrix products  35.9 us (9%)
  between operations  14.3 us (4%)
    all_gather x1, waiting for transfers between devices, on_device(): gathered = lax.all_gather(mixer, 'tp', axis=1, tiled=True)  102 us
    all_gather x1, waiting for transfers between devices, on_device(): shard_rows = lax.all_gather(qkv_weight, 'ctx', axis=0, tiled=True)  74.5 us
    ppermute x9, waiting for transfers between devices, from_behind(): lax.ppermute(value, axis, [(source, source + steps) for source in range(l...  45.3 us
    ppermute x9, starting transfers between devices, from_behind(): lax.ppermute(value, axis, [(source, source + steps) for source in range(l...  37 us
    reshape x1, local copies, waits for them, and re-layouts, local_modal_conv(): jnp.einsum('ts,qsk->qtk', tri, lifted, precision=PRECISE)  19.9 us
    dot_general x1, matrix products, local_modal_conv(): jnp.einsum('ts,qsk->qtk', tri, lifted, precision=PRECISE)  14.5 us
    reduce_sum x1, other arithmetic, local_modal_conv(): intra = jnp.sum(states * mixing[None, None], axis=2)  10.5 us
    mul x1, other arithmetic, local_modal_conv(): up[None] * blocks[:, :, None, :]  9.46 us
  transfers between devices with their start and end apart: 11, of which 9 were waited for; matrix products, arithmetic and copies ran while one was open for 7% of the time, Pallas kernels for 0%

commit v1 on v0

--- a/solution.py
+++ b/solution.py
@@ -89,7 +89,9 @@
     filtered = (intra + carried).reshape(tok_dev, channels) + skip_gain[None] * gated
     filtered = to_bf16_grid(filtered)
     mixer = (short_conv[:, 0] * filtered).astype(jnp.bfloat16)
-    gathered = lax.all_gather(mixer, "tp", axis=1, tiled=True)
+    gathered = jnp.concatenate(
+        lax.all_to_all(jnp.stack([mixer] * lax.axis_size("tp")), "tp", 0, 0), axis=1
+    )
     as_float = gathered.astype(jnp.float32)
     inverse = lax.rsqrt(jnp.mean(as_float * as_float, axis=1, keepdims=True) + EPSILON)
     normed = (as_float * inverse * norm_gain[None]).astype(jnp.bfloat16)

time: 398 us -> 289 us (0.73)
  waiting for transfers between devices: 222 us -> 88.5 us
  starting transfers between devices: 37.1 us -> 48.1 us
  local copies, waits for them, and re-layouts: 44.1 us -> 53.2 us
  other arithmetic: 43.3 us -> 47.5 us
    all_gather x1 -> x0, waiting for transfers between devices: 102 us -> none  [on_device(): gathered = lax.all_gather(mixer, 'tp', axis=1, tiled=True)]
    all_gather x1, waiting for transfers between devices: 74.5 us -> 0.01 us  [on_device(): shard_rows = lax.all_gather(qkv_weight, 'ctx', axis=0, tiled=True)]
    all_to_all x0 -> x1, waiting for transfers between devices: none -> 37.2 us  [on_device(): lax.all_to_all(jnp.stack([mixer] * lax.axis_size('tp')), 'tp', 0, 0)]
    ppermute x9, waiting for transfers between devices: 45.3 us -> 51.3 us  [from_behind(): lax.ppermute(value, axis, [(source, source + steps) for source in range(l...]
    ppermute x9, starting transfers between devices: 37 us -> 42.7 us  [from_behind(): lax.ppermute(value, axis, [(source, source + steps) for source in range(l...]
    all_to_all x0 -> x1, starting transfers between devices: none -> 5.36 us  [on_device(): lax.all_to_all(jnp.stack([mixer] * lax.axis_size('tp')), 'tp', 0, 0)]
    convert_element_type x0 -> x1, other arithmetic: none -> 4.11 us  [on_device(): normed = (as_float * inverse * norm_gain[None]).astype(jnp.bfloat16)]
  transfers between devices with their start and end apart: 11 -> 11, of which waited for: 9 -> 8; matrix products, arithmetic and copies ran while one was open for 7% -> 41% of each run, Pallas kernels for 0% -> 0%
where the time goes in v1:
time: 289 us; the launch traced here: 284 us
  waiting for transfers between devices  88.5 us (31%)
  local copies, waits for them, and re-layouts  53.2 us (18%)
  starting transfers between devices  48.1 us (17%)
  other arithmetic  47.5 us (16%)
  matrix products  32.7 us (11%)
  between operations  14.3 us (5%)
    ppermute x9, waiting for transfers between devices, from_behind(): lax.ppermute(value, axis, [(source, source + steps) for source in range(l...  51.3 us
    ppermute x9, starting transfers between devices, from_behind(): lax.ppermute(value, axis, [(source, source + steps) for source in range(l...  42.7 us
    all_to_all x1, waiting for transfers between devices, on_device(): lax.all_to_all(jnp.stack([mixer] * lax.axis_size('tp')), 'tp', 0, 0)  37.2 us
    reshape x1, local copies, waits for them, and re-layouts, local_modal_conv(): jnp.einsum('ts,qsk->qtk', tri, lifted, precision=PRECISE)  20.1 us
    dot_general x1, matrix products, local_modal_conv(): jnp.einsum('ts,qsk->qtk', tri, lifted, precision=PRECISE)  14.5 us
    reduce_sum x1, other arithmetic, local_modal_conv(): intra = jnp.sum(states * mixing[None, None], axis=2)  10.6 us
    mul x1, other arithmetic, local_modal_conv(): up[None] * blocks[:, :, None, :]  9.47 us
    dot_general x1, matrix products, on_device(): jnp.dot(normed, flat_rows, preferred_element_type=jnp.float32)  7.52 us
  transfers between devices with their start and end apart: 11, of which 8 were waited for; matrix products, arithmetic and copies ran while one was open for 41% of the time, Pallas kernels for 0%

profile of v1, /device:TPU:105, one launch (start us, length us, event | category | flops | bytes accessed | tf_op | source)
XLA Modules:
  0.0 284.4 jit_solution(16225001903110963648)
XLA Ops:
  8.0 3.7 %collective-permute-start = (bf16[6,3,512]{2,0,1:T(8,128)(2,1)S(1)}, bf16[6,3,512]{2,0,1:T(8,128)(2,1)S(1)}, u32[]{:S(2)}, u32[]{:S(2)}) collective-permute-start(bf16[6,3,512]{2,0,1:T(8,128)(2,1)S(1)} %slice.102), channel_id=1, source_target_pairs={{0,8},{8,16},{16,24},{24,32},{32,40},{40,48},{48,56},{56,64},{64,7... | collective-permute-start | bytes 55304 | tf_op jit(solution)/shard_map/ppermute | solution.py:23
  17.1 4.6 %multiply_exponential_fusion = f32[128,8192]{0,1:T(8,128)} fusion(f32[8192]{0:T(1024)S(1)} %bitcast.163, f32[128]{0:T(128)S(1)} %iota_add_fusion), kind=kLoop, calls=%fused_computation.12 | loop fusion | flops 1048576 | bytes 4227584 | tf_op jit(solution)/shard_map/exp | solution.py:32
  21.7 3.5 %multiply_exponential_fusion.1 = f32[128,16,512]{0,1,2:T(8,128)} fusion(f32[16,512]{0,1:T(8,128)S(1)} %copy.51, f32[128]{0:T(128)S(1)} %fusion.81), kind=kLoop, calls=%fused_computation.13 | loop fusion | flops 1048576 | bytes 4227584 | tf_op jit(solution)/shard_map/exp | solution.py:33
  25.3 5.7 %copy.52 = f32[128,16,512]{2,1,0:T(8,128)} copy(f32[128,16,512]{0,1,2:T(8,128)} %multiply_exponential_fusion.1) | data formatting | bytes 8388608 | tf_op jit(solution)/shard_map/exp | solution.py:33
  31.5 2.6 fusion.7
  35.4 2.5 copy.53
  37.9 9.5 %bitcast_multiply_fusion = f32[4,128,8192]{1,2,0:T(8,128)} fusion(f32[4,128,512]{1,2,0:T(8,128)} %copy.53, f32[128,8192]{0,1:T(8,128)} %multiply_exponential_fusion), kind=kLoop, calls=%fused_computation | loop fusion | flops 4194304 | bytes 22020096 | tf_op jit(solution)/shard_map/mul | solution.py:37
  47.4 14.5 %fusion.71 = f32[4,8192,128]{2,1,0:T(8,128)} fusion(f32[4,128,8192]{1,2,0:T(8,128)} %bitcast_multiply_fusion), kind=kOutput, calls=%fused_computation.99 | convolution fusion | flops 6442467328 | bytes 33554432 | tf_op jit(solution)/shard_map/ts,qsk->qtk/dot_general | solution.py:38
  61.8 20.1 %copy.54 = f32[4,128,16,512]{3,2,1,0:T(8,128)} copy(f32[4,128,16,512]{1,3,2,0:T(8,128)} %bitcast.155) | data formatting | bytes 33554432 | tf_op jit(solution)/shard_map/reshape | solution.py:38
  81.9 10.6 %multiply_reduce_fusion = (f32[4,128,512]{2,1,0:T(8,128)}, f32[4,128,16,512]{3,2,1,0:T(8,128)S(1)}) fusion(f32[16,512]{1,0:T(8,128)S(1)} %sqrt_multiply_fusion, f32[4,128,16,512]{3,2,1,0:T(8,128)} %copy.54, f32[128,16,512]{2,1,0:T(8,128)} %copy.52), kind=kLoop, calls=%fused_computation.1 | loop fusion | flops 12320768 | bytes 38830080 | tf_op jit(solution)/shard_map/reduce_sum | solution.py:42
  96.2 4.0 %collective-permute-start.2 = (f32[16,512]{1,0:T(8,128)S(1)}, f32[16,512]{1,0:T(8,128)S(1)}, u32[]{:S(2)}, u32[]{:S(2)}) collective-permute-start(f32[16,512]{1,0:T(8,128)S(1)} %collective-permute-done.1), channel_id=1, source_target_pairs={{0,8},{8,16},{16,24},{24,32},{32,40},{40,48},{48,56},{56,64},{64,7... | collective-permute-start | bytes 98312 | tf_op jit(solution)/shard_map/ppermute | solution.py:23
  100.3 2.7 collective-permute-done.2
  104.9 6.1 %collective-permute-done.3 = f32[16,512]{1,0:T(8,128)S(1)} collective-permute-done((f32[16,512]{1,0:T(8,128)S(1)}, f32[16,512]{1,0:T(8,128)S(1)}, u32[]{:S(2)}, u32[]{:S(2)}) %collective-permute-start.3) | collective-permute-done | bytes 32800 | tf_op jit(solution)/shard_map/ppermute | solution.py:23
  111.0 5.1 %collective-permute-start.4 = (f32[16,512]{1,0:T(8,128)S(1)}, f32[16,512]{1,0:T(8,128)S(1)}, u32[]{:S(2)}, u32[]{:S(2)}) collective-permute-start(f32[16,512]{1,0:T(8,128)S(1)} %multiply_add_fusion.3), channel_id=1, source_target_pairs={{0,32},{8,40},{16,48},{24,56},{32,64},{40,72},{48,80},{56,88},{64,... | collective-permute-start | bytes 98312 | tf_op jit(solution)/shard_map/ppermute | solution.py:23
  116.1 2.8 %collective-permute-done.4 = f32[16,512]{1,0:T(8,128)S(1)} collective-permute-done((f32[16,512]{1,0:T(8,128)S(1)}, f32[16,512]{1,0:T(8,128)S(1)}, u32[]{:S(2)}, u32[]{:S(2)}) %collective-permute-start.4) | collective-permute-done | bytes 32800 | tf_op jit(solution)/shard_map/ppermute | solution.py:23
  118.9 8.7 %collective-permute-start.5 = (f32[16,512]{1,0:T(8,128)S(1)}, f32[16,512]{1,0:T(8,128)S(1)}, u32[]{:S(2)}, u32[]{:S(2)}) collective-permute-start(f32[16,512]{1,0:T(8,128)S(1)} %multiply_add_fusion.2), channel_id=1, source_target_pairs={{0,64},{8,72},{16,80},{24,88},{32,96},{40,104},{48,112},{56,120},{... | collective-permute-start | bytes 98312 | tf_op jit(solution)/shard_map/ppermute | solution.py:23
  128.7 4.9 %collective-permute-start.6 = (f32[16,512]{1,0:T(8,128)S(1)}, f32[16,512]{1,0:T(8,128)}, u32[]{:S(2)}, u32[]{:S(2)}) collective-permute-start(f32[16,512]{1,0:T(8,128)S(1)} %multiply_add_fusion.1), channel_id=1, source_target_pairs={{0,128},{8,136},{16,144},{24,152},{32,160},{40,168},{48,176},{56,1... | collective-permute-start | bytes 98312 | tf_op jit(solution)/shard_map/ppermute | solution.py:23
  134.4 2.6 copy.57
  139.3 2.2 copy.56
  141.5 7.4 %fusion.28 = f32[4,128,512]{1,0,2:T(4,128)} fusion(f32[4,128,512]{1,0,2:T(4,128)} %copy.57, f32[4,16,512]{1,0,2:T(4,128)} %copy.56, f32[16,512]{0,1:T(8,128)} %copy.55, f32[128]{0:T(128)S(1)} %add_negate_fusion, f32[16,512]{0,1:T(8,128)S(1)} %copy.51), kind=kOutput, calls=%fused_computation.48 | convolution fusion | flops 52690944 | bytes 2294272 | tf_op jit(solution)/shard_map/lnc,qnc->qlc/dot_general | solution.py:88
  149.0 2.5 copy.77
  151.5 2.5 fusion.40
  155.3 2.3 stack.43
  157.6 5.4 %all-to-all-start = ((bf16[8,512,512]{1,2,0:T(8,128)(2,1)}), bf16[8,512,512]{1,2,0:T(8,128)(2,1)}, u32[]{:S(2)}, u32[]{:S(2)}) async-start(bf16[8,512,512]{1,2,0:T(8,128)(2,1)} %stack.43), calls=%async_computation | async-start | bytes 8388608 | tf_op jit(solution)/shard_map/all_to_all | solution.py:93
  163.1 37.2 %all-to-all-done = bf16[8,512,512]{1,2,0:T(8,128)(2,1)} async-done(((bf16[8,512,512]{1,2,0:T(8,128)(2,1)}), bf16[8,512,512]{1,2,0:T(8,128)(2,1)}, u32[]{:S(2)}, u32[]{:S(2)}) %all-to-all-start) | async-done | bytes 4194336 | tf_op jit(solution)/shard_map/all_to_all | solution.py:93
  200.3 3.1 %fusion = f32[512]{0:T(512)S(1)} fusion(bf16[8,512,512]{1,2,0:T(8,128)(2,1)} %all-to-all-done), kind=kLoop, calls=%fused_computation.4 | loop fusion | flops 6290944 | bytes 4196352 | tf_op jit(solution)/shard_map/reduce_sum | solution.py:96
  203.4 4.1 %fusion.2 = bf16[8,512,512]{1,2,0:T(8,128)(2,1)} fusion(bf16[8,512,512]{1,2,0:T(8,128)(2,1)} %all-to-all-done, f32[8,512]{1,0:T(8,128)S(1)} %mul.344, f32[512]{0:T(512)S(1)} %add_rsqrt_fusion), kind=kLoop, calls=%fused_computation.6 | loop fusion | flops 8388608 | bytes 8407040 | tf_op jit(solution)/shard_map/convert_element_type | solution.py:97
  207.5 7.5 %convolution_convert_fusion = bf16[512,768]{1,0:T(8,128)(2,1)S(1)} fusion(bf16[512,4096]{0,1:T(8,128)(2,1)} %bitcast.156, bf16[4096,768]{0,1:T(8,128)(2,1)} %bitcast.165), kind=kOutput, calls=%fused_computation.46 | convolution fusion | flops 3221618688 | bytes 11272192 | tf_op jit(solution)/shard_map/dot_general | solution.py:99
  215.9 9.5 %collective-permute-start.7 = (bf16[512,512]{1,0:T(8,128)(2,1)}, bf16[512,512]{1,0:T(8,128)(2,1)}, u32[]{:S(2)}, u32[]{:S(2)}) collective-permute-start(bf16[512,512]{1,0:T(8,128)(2,1)} %slice.148), channel_id=1, source_target_pairs={{0,8},{8,16},{16,24},{24,32},{32,40},{40,48},{48,56},{56,64},{64,7... | collective-permute-start | bytes 1572872 | tf_op jit(solution)/shard_map/ppermute | solution.py:23
  225.4 2.7 collective-permute-start.8
  229.7 2.2 collective-permute-done.7
  233.1 35.5 %collective-permute-done.8 = bf16[512,512]{1,0:T(8,128)(2,1)} collective-permute-done((bf16[512,512]{1,0:T(8,128)(2,1)}, bf16[512,512]{1,0:T(8,128)(2,1)}, u32[]{:S(2)}, u32[]{:S(2)}) %collective-permute-start.8) | collective-permute-done | bytes 524320 | tf_op jit(solution)/shard_map/ppermute | solution.py:23
  (67 shorter events, 31.6 us)
Async XLA Ops:
  7.2 200.4 %all-gather.2.cloned.1.call-start = ((), (), s32[]{:S(2)}) async-start(), calls=%async_computation.1 | async-start | bytes 6488064 | tf_op jit(solution)/shard_map/all_gather | solution.py:58
  8.0 23.1 %collective-permute-start = (bf16[6,3,512]{2,0,1:T(8,128)(2,1)S(1)}, bf16[6,3,512]{2,0,1:T(8,128)(2,1)S(1)}, u32[]{:S(2)}, u32[]{:S(2)}) collective-permute-start(bf16[6,3,512]{2,0,1:T(8,128)(2,1)S(1)} %slice.102), channel_id=1, source_target_pairs={{0,8},{8,16},{16,24},{24,32},{32,40},{40,48},{48,56},{56,64},{64,7... | collective-permute-start | bytes 55304 | tf_op jit(solution)/shard_map/ppermute | solution.py:23
  25.3 5.8 %copy-start.1 = (bf16[512,3,512]{2,0,1:T(8,128)(2,1)S(1)}, bf16[512,3,512]{2,0,1:T(8,128)(2,1)}, u32[]{:S(2)}) copy-start(bf16[512,3,512]{2,0,1:T(8,128)(2,1)} %param.7) | copy-start | bytes 4718596
  81.9 10.6 %copy-start = (f32[16,512]{1,0:T(8,128)S(1)}, f32[16,512]{1,0:T(8,128)}, u32[]{:S(2)}) copy-start(f32[16,512]{1,0:T(8,128)} %param.9) | copy-start | bytes 98308
  93.1 3.1 %collective-permute-start.1 = (f32[16,512]{1,0:T(8,128)S(1)}, f32[16,512]{1,0:T(8,128)S(1)}, u32[]{:S(2)}, u32[]{:S(2)}) collective-permute-start(f32[16,512]{1,0:T(8,128)S(1)} %get-tuple-element.13), channel_id=1, source_target_pairs={{0,8},{8,16},{16,24},{24,32},{32,40},{40,48},{48,56},{56,64},{64,7... | collective-permute-start | bytes 98312 | tf_op jit(solution)/shard_map/ppermute | solution.py:23
  96.2 6.7 %collective-permute-start.2 = (f32[16,512]{1,0:T(8,128)S(1)}, f32[16,512]{1,0:T(8,128)S(1)}, u32[]{:S(2)}, u32[]{:S(2)}) collective-permute-start(f32[16,512]{1,0:T(8,128)S(1)} %collective-permute-done.1), channel_id=1, source_target_pairs={{0,8},{8,16},{16,24},{24,32},{32,40},{40,48},{48,56},{56,64},{64,7... | collective-permute-start | bytes 98312 | tf_op jit(solution)/shard_map/ppermute | solution.py:23
  103.0 8.0 %collective-permute-start.3 = (f32[16,512]{1,0:T(8,128)S(1)}, f32[16,512]{1,0:T(8,128)S(1)}, u32[]{:S(2)}, u32[]{:S(2)}) collective-permute-start(f32[16,512]{1,0:T(8,128)S(1)} %multiply_add_fusion.4), channel_id=1, source_target_pairs={{0,16},{8,24},{16,32},{24,40},{32,48},{40,56},{48,64},{56,72},{64,... | collective-permute-start | bytes 98312 | tf_op jit(solution)/shard_map/ppermute | solution.py:23
  111.0 8.0 %collective-permute-start.4 = (f32[16,512]{1,0:T(8,128)S(1)}, f32[16,512]{1,0:T(8,128)S(1)}, u32[]{:S(2)}, u32[]{:S(2)}) collective-permute-start(f32[16,512]{1,0:T(8,128)S(1)} %multiply_add_fusion.3), channel_id=1, source_target_pairs={{0,32},{8,40},{16,48},{24,56},{32,64},{40,72},{48,80},{56,88},{64,... | collective-permute-start | bytes 98312 | tf_op jit(solution)/shard_map/ppermute | solution.py:23
  118.9 9.7 %collective-permute-start.5 = (f32[16,512]{1,0:T(8,128)S(1)}, f32[16,512]{1,0:T(8,128)S(1)}, u32[]{:S(2)}, u32[]{:S(2)}) collective-permute-start(f32[16,512]{1,0:T(8,128)S(1)} %multiply_add_fusion.2), channel_id=1, source_target_pairs={{0,64},{8,72},{16,80},{24,88},{32,96},{40,104},{48,112},{56,120},{... | collective-permute-start | bytes 98312 | tf_op jit(solution)/shard_map/ppermute | solution.py:23
  128.7 8.3 %collective-permute-start.6 = (f32[16,512]{1,0:T(8,128)S(1)}, f32[16,512]{1,0:T(8,128)}, u32[]{:S(2)}, u32[]{:S(2)}) collective-permute-start(f32[16,512]{1,0:T(8,128)S(1)} %multiply_add_fusion.1), channel_id=1, source_target_pairs={{0,128},{8,136},{16,144},{24,152},{32,160},{40,168},{48,176},{56,1... | collective-permute-start | bytes 98312 | tf_op jit(solution)/shard_map/ppermute | solution.py:23
  141.5 10.0 %copy-start.5 = (f32[512]{0:T(512)S(1)}, f32[512]{0:T(512)}, u32[]{:S(2)}) copy-start(f32[512]{0:T(512)} %param.11) | copy-start | bytes 6148
  157.6 5.4 %copy-start.4 = (f32[4096]{0:T(1024)S(1)}, f32[4096]{0:T(1024)}, u32[]{:S(2)}) copy-start(f32[4096]{0:T(1024)} %param.12) | copy-start | bytes 49156
  157.6 42.7 %all-to-all-start = ((bf16[8,512,512]{1,2,0:T(8,128)(2,1)}), bf16[8,512,512]{1,2,0:T(8,128)(2,1)}, u32[]{:S(2)}, u32[]{:S(2)}) async-start(bf16[8,512,512]{1,2,0:T(8,128)(2,1)} %stack.43), calls=%async_computation | async-start | bytes 8388608 | tf_op jit(solution)/shard_map/all_to_all | solution.py:93
  215.9 16.0 %collective-permute-start.7 = (bf16[512,512]{1,0:T(8,128)(2,1)}, bf16[512,512]{1,0:T(8,128)(2,1)}, u32[]{:S(2)}, u32[]{:S(2)}) collective-permute-start(bf16[512,512]{1,0:T(8,128)(2,1)} %slice.148), channel_id=1, source_target_pairs={{0,8},{8,16},{16,24},{24,32},{32,40},{40,48},{48,56},{56,64},{64,7... | collective-permute-start | bytes 1572872 | tf_op jit(solution)/shard_map/ppermute | solution.py:23
  225.4 43.2 %collective-permute-start.8 = (bf16[512,512]{1,0:T(8,128)(2,1)}, bf16[512,512]{1,0:T(8,128)(2,1)}, u32[]{:S(2)}, u32[]{:S(2)}) collective-permute-start(bf16[512,512]{1,0:T(8,128)(2,1)} %slice.148), channel_id=1, source_target_pairs={{0,16},{8,24},{16,32},{24,40},{32,48},{40,56},{48,64},{56,72},{64,... | collective-permute-start | bytes 1572872 | tf_op jit(solution)/shard_map/ppermute | solution.py:23
  272.2 0.9 copy-start.2
  275.2 1.0 copy-start.3
Sparse Core Ops, SparseCore 0:
  13.5 74.2 all-gather.1
